TPU v7x, 128 devices: a whole 4x4x4 slice. The times are simulated.
128 devices in a mesh: dp: 16 (over y, x), expert: 8 (over z, core).
Axes of the slice: x: 4, y: 4, z: 4, core: 2. Of those that a mesh axis runs over, the one named last changes fastest.
Arguments:
- tokens: bfloat16 [4096, 4096], P('dp', 'expert'), may hold values from -100 to 100
- w_gate: bfloat16 [8, 4096, 14336], P('expert', None, 'dp'), may hold values from -0.09375 to 0.09375
- w_up: bfloat16 [8, 4096, 14336], P('expert', None, 'dp'), may hold values from -0.09375 to 0.09375
- w_down: bfloat16 [8, 14336, 4096], P('expert', 'dp'), may hold values from -0.046875 to 0.046875
- pick_block: int32 [8, 8], replicated, may hold values from 0 to 3
- pick_live: int32 [8, 8], replicated, may hold values from 0 to 1, as said below
- combine_weight: float32 [8, 8], replicated, may hold values from 0.25 to 1
Outputs:
- combined: bfloat16 [4096, 4096], P('dp', 'expert')
Inputs may be any that keep to these rules, and one draw needn't show every extreme that they name: `pick_live`: each expert takes at least one block, and some expert takes a block from every pair of dp rows.
All inputs are finite; a program needn't handle non-finite values.
Results may differ from a plain program's by a relative error of at most 0.02.
Values may be sent and summed in bfloat16 or wider, within the bound.
A program may use at most 128 MiB of HBM per device.

v0:
```python
import jax
import jax.numpy as jnp
from jax import lax
from jax.sharding import PartitionSpec as P

BLOCK = 128


def from_partner(value, axis, stride):
    return lax.ppermute(value, axis, [(i, i ^ 1 << stride) for i in range(lax.axis_size(axis))])


def rms_normalize(values, square_sums, model_width):
    values_f32 = values.astype(jnp.float32)
    inv_rms = lax.rsqrt(square_sums / model_width + 1e-05)
    return (values_f32 * inv_rms[:, None]).astype(jnp.bfloat16)


def on_device(tokens, w_gate, w_up, w_down, pick_block, pick_live, combine_weight):
    expert_count = lax.axis_size("expert")
    features_dev = tokens.shape[1]
    model_width = features_dev * expert_count
    blocks_here = tokens.shape[0] // BLOCK
    half_rows = BLOCK // 2
    row_index = lax.axis_index("dp")
    half_bit = row_index % 2
    pair_index = row_index // 2
    tokens_f32 = tokens.astype(jnp.float32)
    square_sums = lax.psum(jnp.sum(tokens_f32 * tokens_f32, axis=1), "expert")
    source = rms_normalize(tokens, square_sums, model_width)
    picked = lax.dynamic_index_in_dim(pick_block, pair_index, axis=1, keepdims=False)
    live_flags = lax.dynamic_index_in_dim(pick_live, pair_index, axis=1, keepdims=False)
    weights_here = lax.dynamic_index_in_dim(combine_weight, pair_index, axis=1, keepdims=False)
    owned_here = (live_flags == 1) & (picked // blocks_here == half_bit)
    local_block = picked % blocks_here
    blocks = source.reshape(blocks_here, BLOCK, features_dev)
    chosen = jnp.take(blocks, local_block, axis=0)
    chosen = jnp.where(owned_here[:, None, None], chosen, jnp.zeros((), jnp.bfloat16))
    arrived = lax.all_to_all(chosen, "expert", split_axis=0, concat_axis=2, tiled=True)[0]
    outgoing = lax.dynamic_slice_in_dim(arrived, (1 - half_bit) * half_rows, half_rows, 0)
    partner = from_partner(outgoing, "dp", 0)
    own_half = lax.dynamic_slice_in_dim(arrived, half_bit * half_rows, half_rows, 0)
    merged = own_half + partner
    gate_weights = w_gate[0]
    up_weights = w_up[0]
    down_weights = w_down[0]
    rows_piece = lax.all_gather(merged, "dp", axis=0, tiled=True)
    gate_proj = jnp.dot(rows_piece, gate_weights, preferred_element_type=jnp.float32)
    up_proj = jnp.dot(rows_piece, up_weights, preferred_element_type=jnp.float32)
    hidden = (jax.nn.silu(gate_proj) * up_proj).astype(jnp.bfloat16)
    partial_value = jnp.dot(hidden, down_weights, preferred_element_type=jnp.float32).astype(
        jnp.bfloat16
    )
    summed = lax.psum_scatter(
        lax.optimization_barrier(partial_value).astype(jnp.float32).astype(jnp.bfloat16),
        "dp",
        scatter_dimension=0,
        tiled=True,
    )
    spread = lax.all_to_all(summed[:, None, :], "expert", split_axis=2, concat_axis=1, tiled=True)
    other_half = from_partner(spread, "dp", 0)
    assembled = jnp.where(
        half_bit == 0,
        jnp.concatenate([spread, other_half], axis=0),
        jnp.concatenate([other_half, spread], axis=0),
    )
    slot_match = local_block[None, :] == jnp.arange(blocks_here, dtype=jnp.int32)[:, None]
    combine_coef = jnp.where(
        slot_match & owned_here[None, :], weights_here[None, :], jnp.zeros((), jnp.float32)
    )
    combined = jnp.einsum("le,red->lrd", combine_coef, assembled.astype(jnp.float32))
    return combined.astype(jnp.bfloat16).reshape(blocks_here * BLOCK, features_dev)


def solution(mesh):
    in_specs = (
        P("dp", "expert"),
        P("expert", None, "dp"),
        P("expert", None, "dp"),
        P("expert", "dp", None),
        P(),
        P(),
        P(),
    )
    out_specs = P("dp", "expert")
    return jax.shard_map(
        on_device, mesh=mesh, in_specs=in_specs, out_specs=out_specs, check_vma=False
    )
```

profile of v0, /device:TPU:0, one launch (start us, length us, event | category | flops | bytes accessed | tf_op | source)
XLA Modules:
  0.0 329.2 jit_solution(12364163355996505817)
XLA Ops:
  6.5 0.9 dynamic-slice_reduce_fusion.1
  7.5 1.1 fusion.12
  8.6 16.0 %psum.7 = f32[256]{0:T(256)S(1)} all-reduce(f32[256]{0:T(256)S(1)} %fusion.12), channel_id=1, replica_groups=mesh['dp'=16,'expert'=8] {'expert'}, use_global_device_ids=true, to_apply=%region_1.2 | all-reduce | flops 256 | bytes 2048 | tf_op jit(solution)/shard_map/psum | solution.py:29
  24.5 1.1 fusion.13
  25.6 0.9 fusion.15
  27.2 1.2 select_select_fusion
  28.4 3.6 %all-to-all-start = ((bf16[8,128,512]{2,1,0:T(8,128)(2,1)}), bf16[8,128,512]{2,1,0:T(8,128)(2,1)S(1)}, u32[]{:S(2)}, u32[]{:S(2)}) async-start(bf16[8,128,512]{2,1,0:T(8,128)(2,1)} %select_select_fusion), calls=%async_computation | async-start | bytes 2097152 | tf_op jit(solution)/shard_map/all_to_all | solution.py:39
  32.0 15.8 %all-to-all-done = bf16[8,128,512]{2,1,0:T(8,128)(2,1)S(1)} async-done(((bf16[8,128,512]{2,1,0:T(8,128)(2,1)}), bf16[8,128,512]{2,1,0:T(8,128)(2,1)S(1)}, u32[]{:S(2)}, u32[]{:S(2)}) %all-to-all-start) | async-done | bytes 1048608 | tf_op jit(solution)/shard_map/all_to_all | solution.py:39
  49.5 1.6 collective-permute-start
  51.4 11.6 %collective-permute-done = bf16[64,4096]{1,0:T(8,128)(2,1)S(1)} collective-permute-done((bf16[64,4096]{1,0:T(8,128)(2,1)S(1)}, bf16[64,4096]{1,0:T(8,128)(2,1)S(1)}, u32[]{:S(2)}, u32[]{:S(2)}) %collective-permute-start) | collective-permute-done | bytes 524320 | tf_op jit(solution)/shard_map/ppermute | solution.py:10
  63.0 1.0 add.73
  64.2 70.0 %all-gather.2.cloned.1.call-done = bf16[1024,4096]{1,0:T(8,128)(2,1)} async-done(((bf16[64,4096]{1,0:T(8,128)(2,1)}), bf16[1024,4096]{1,0:T(8,128)(2,1)}) %all-gather.2.cloned.1.call-update) | async-done | bytes 8388624 | tf_op jit(solution)/shard_map/all_gather | solution.py:47
  134.3 12.5 %fusion.1 = f32[1024,896]{1,0:T(8,128)S(1)} fusion(bf16[1024,4096]{1,0:T(8,128)(2,1)} %all-gather.2.cloned.1.call-done, bf16[1,4096,896]{2,1,0:T(8,128)(2,1)} %param.9), kind=kOutput, calls=%fused_computation.3 | convolution fusion | flops 7516192768 | bytes 19398656 | tf_op jit(solution)/shard_map/dot_general | solution.py:49
  146.8 15.1 %fusion.3 = f32[1024,896]{1,0:T(8,128)S(1)} fusion(bf16[1024,4096]{1,0:T(8,128)(2,1)S(1)} %copy-done.1, bf16[1,4096,896]{2,1,0:T(8,128)(2,1)} %param.8), kind=kOutput, calls=%fused_computation.5 | convolution fusion | flops 7516192768 | bytes 19398656 | tf_op jit(solution)/shard_map/dot_general | solution.py:48
  161.9 14.1 %convolution_convert_fusion = bf16[1024,4096]{1,0:T(8,128)(2,1)} fusion(bf16[1,896,4096]{2,1,0:T(8,128)(2,1)} %param.10, f32[1024,896]{1,0:T(8,128)S(1)} %fusion.1, f32[1024,896]{1,0:T(8,128)S(1)} %fusion.3), kind=kOutput, calls=%fused_computation.1 | convolution fusion | flops 7525892096 | bytes 23068672 | tf_op jit(solution)/shard_map/dot_general | solution.py:51
  176.0 84.8 %reduce-scatter.2.cloned.1.call-done = bf16[64,4096]{1,0:T(8,128)(2,1)} async-done(((bf16[1024,4096]{1,0:T(8,128)(2,1)}), bf16[64,4096]{1,0:T(8,128)(2,1)}) %reduce-scatter.2.cloned.1.call-update) | async-done | bytes 524304 | tf_op jit(solution)/shard_map/reduce_scatter | solution.py:54
  260.7 4.9 %copy.30 = bf16[64,1,4096]{0,1,2:T(2,128)(2,1)S(1)} copy(bf16[64,1,4096]{2,0,1:T(8,128)(2,1)} %bitcast.33) | data formatting | bytes 1048576 | tf_op jit(solution)/shard_map/broadcast_in_dim | solution.py:60
  266.1 22.6 %reduce.10 = bf16[4096,64]{1,0:T(8,128)(2,1)S(1)} reduce(bf16[4096,1,64]{2,1,0:T(2,128)(2,1)S(1)} %bitcast.29, bf16[]{:T(256)} %broadcast.170), dimensions={1}, to_apply=%bitcast.23.reduce_sub_computation | reduce | bytes 1048578
  289.5 14.6 %all_to_all.27 = bf16[8,2,16384]{2,1,0:T(2,128)(2,1)S(1)} all-to-all(bf16[8,2,16384]{2,1,0:T(2,128)(2,1)S(1)} %reshape.126), channel_id=1, replica_groups=mesh['dp'=16,'expert'=8] {'expert'}, dimensions={0} | all-to-all | bytes 1048576 | tf_op jit(solution)/shard_map/all_to_all | solution.py:60
  304.1 1.2 reshape.127
  305.4 2.3 copy.31
  307.8 1.5 collective-permute-start.1
  309.5 11.7 %collective-permute-done.1 = bf16[64,8,512]{2,1,0:T(8,128)(2,1)S(1)} collective-permute-done((bf16[64,8,512]{2,1,0:T(8,128)(2,1)S(1)}, bf16[64,8,512]{2,1,0:T(8,128)(2,1)S(1)}, u32[]{:S(2)}, u32[]{:S(2)}) %collective-permute-start.1) | collective-permute-done | bytes 524320 | tf_op jit(solution)/shard_map/ppermute | solution.py:10
  321.6 0.7 copy.32
  (22 shorter events, 5.0 us)
Async XLA Ops:
  6.5 302.8 %copy-start = (f32[8,8]{1,0:T(8,128)S(1)}, f32[8,8]{1,0:T(8,128)}, u32[]{:S(2)}) copy-start(f32[8,8]{1,0:T(8,128)} %param.13) | copy-start | bytes 772
  28.4 19.4 %all-to-all-start = ((bf16[8,128,512]{2,1,0:T(8,128)(2,1)}), bf16[8,128,512]{2,1,0:T(8,128)(2,1)S(1)}, u32[]{:S(2)}, u32[]{:S(2)}) async-start(bf16[8,128,512]{2,1,0:T(8,128)(2,1)} %select_select_fusion), calls=%async_computation | async-start | bytes 2097152 | tf_op jit(solution)/shard_map/all_to_all | solution.py:39
  31.9 102.4 %all-gather.2.cloned.1.call-start = ((), (), s32[]{:S(2)}) async-start(), calls=%async_computation.3 | async-start | bytes 8912896 | tf_op jit(solution)/shard_map/all_gather | solution.py:47
  49.5 13.5 %collective-permute-start = (bf16[64,4096]{1,0:T(8,128)(2,1)S(1)}, bf16[64,4096]{1,0:T(8,128)(2,1)S(1)}, u32[]{:S(2)}, u32[]{:S(2)}) collective-permute-start(bf16[64,4096]{1,0:T(8,128)(2,1)S(1)} %copy.29), channel_id=1, source_target_pairs={{0,8},{8,0},{16,24},{24,16},{32,40},{40,32},{48,56},{56,48},{64,72... | collective-permute-start | bytes 1572872 | tf_op jit(solution)/shard_map/ppermute | solution.py:10
  64.0 196.7 %reduce-scatter.2.cloned.1.call-start = ((), (), s32[]{:S(2)}) async-start(), calls=%async_computation.4 | async-start | bytes 8912896 | tf_op jit(solution)/shard_map/reduce_scatter | solution.py:54
  134.3 12.5 %copy-start.1 = (bf16[1024,4096]{1,0:T(8,128)(2,1)S(1)}, bf16[1024,4096]{1,0:T(8,128)(2,1)}, u32[]{:S(2)}) copy-start(bf16[1024,4096]{1,0:T(8,128)(2,1)} %all-gather.2.cloned.1.call-done) | copy-start | bytes 25165828
  307.8 13.4 %collective-permute-start.1 = (bf16[64,8,512]{2,1,0:T(8,128)(2,1)S(1)}, bf16[64,8,512]{2,1,0:T(8,128)(2,1)S(1)}, u32[]{:S(2)}, u32[]{:S(2)}) collective-permute-start(bf16[64,8,512]{2,1,0:T(8,128)(2,1)S(1)} %bitcast.34), channel_id=1, source_target_pairs={{0,8},{8,0},{16,24},{24,16},{32,40},{40,32},{48,56},{56,48},{64,72... | collective-permute-start | bytes 1572872 | tf_op jit(solution)/shard_map/ppermute | solution.py:10
Sparse Core Ops, SparseCore 0:
  64.1 70.0 all-gather.1
  176.1 84.5 reduce-scatter.1
where the time goes:
time: 330 us; the launch traced here: 329 us
  waiting for transfers between devices  194 us (59%)
  matrix products  42.1 us (13%)
  blocking collectives  30.6 us (9%)
  other arithmetic  28.8 us (9%)
  between operations  13.6 us (4%)
  local copies, waits for them, and re-layouts  13.3 us (4%)
  starting transfers between devices  6.86 us (2%)
    reduce_scatter x1, waiting for transfers between devices, on_device(): lax.psum_scatter(lax.optimization_barrier(partial_value).astype(jnp.float...  84.8 us
    all_gather x1, waiting for transfers between devices, on_device(): rows_piece = lax.all_gather(merged, 'dp', axis=0, tiled=True)  70 us
    ppermute x2, waiting for transfers between devices, from_partner(): lax.ppermute(value, axis, [(i, i ^ 1 << stride) for i in range(lax.axis_s...  23.3 us
    unnamed x1, other arithmetic  22.6 us
    psum x1, blocking collectives, on_device(): square_sums = lax.psum(jnp.sum(tokens_f32 * tokens_f32, axis=1), 'expert')  16 us
    all_to_all x1, waiting for transfers between devices, on_device(): lax.all_to_all(chosen, 'expert', split_axis=0, concat_axis=2, tiled=True)[0]  15.8 us
    dot_general x1, matrix products, on_device(): jnp.dot(rows_piece, gate_weights, preferred_element_type=jnp.float32)  15.1 us
    all_to_all x1, blocking collectives, on_device(): lax.all_to_all(summed[:, None, :], 'expert', split_axis=2, concat_axis=1,...  14.6 us
  transfers between devices with their start and end apart: 5, of which 5 were waited for; matrix products, arithmetic and copies ran while one was open for 0% of the time, Pallas kernels for 0%

commit v1 on v0

--- a/solution.py
+++ b/solution.py
@@ -1,9 +1,30 @@
+import functools
 import jax
 import jax.numpy as jnp
 from jax import lax
 from jax.sharding import PartitionSpec as P
 
 BLOCK = 128
+
+
+def expand_the_edges(inp, peer_axis):
+    axis_n = lax.axis_size(peer_axis)
+    fields = []
+    for t in range(axis_n):
+        fields.append((t, (t + 1) % axis_n))
+    block_list = []
+    for t in range(axis_n):
+        block_list.append((t, (t - 1) % axis_n))
+    f_now, y2 = ([inp], [inp])
+    for _ in range(axis_n // 2):
+        f_now.append(lax.ppermute(f_now[-1], peer_axis, perm=fields))
+    for _ in range((axis_n - 1) // 2):
+        y2.append(lax.ppermute(y2[-1], peer_axis, block_list))
+    main = jnp.concatenate([*f_now[::-1], *y2[1:]], axis=0)
+    return jnp.roll(main, shift=(lax.axis_index(peer_axis) - axis_n // 2) * inp.shape[0], axis=0)
+
+
+replace_figure = functools.partial(expand_the_edges, peer_axis="dp")
 
 
 def from_partner(value, axis, stride):
@@ -44,7 +65,7 @@
     gate_weights = w_gate[0]
     up_weights = w_up[0]
     down_weights = w_down[0]
-    rows_piece = lax.all_gather(merged, "dp", axis=0, tiled=True)
+    rows_piece = replace_figure(merged)
     gate_proj = jnp.dot(rows_piece, gate_weights, preferred_element_type=jnp.float32)
     up_proj = jnp.dot(rows_piece, up_weights, preferred_element_type=jnp.float32)
     hidden = (jax.nn.silu(gate_proj) * up_proj).astype(jnp.bfloat16)

time: 330 us -> 377 us (1.14)
  starting transfers between devices: 6.86 us -> 47.1 us
  local copies, waits for them, and re-layouts: 13.3 us -> 29.9 us
  waiting for transfers between devices: 194 us -> 188 us
  matrix products: 42.1 us -> 37.9 us
    all_gather x1 -> x0, waiting for transfers between devices: 70 us -> none  [on_device(): rows_piece = lax.all_gather(merged, 'dp', axis=0, tiled=True)]
    ppermute x0 -> x15, waiting for transfers between devices: none -> 69.9 us  [the longest x8 66.6 us: expand_the_edges(): f_now.append(lax.ppermute(f_now[-1], peer_axis, perm=fields))]
    ppermute x0 -> x15, starting transfers between devices: none -> 40.4 us  [the longest x7 38.9 us: expand_the_edges(): y2.append(lax.ppermute(y2[-1], peer_axis, block_list))]
    unnamed x9 -> x66, local copies, waits for them, and re-layouts: 3.01 us -> 19.5 us
    reduce_scatter x1, waiting for transfers between devices: 84.8 us -> 79.3 us  [on_device(): lax.psum_scatter(lax.optimization_barrier(partial_value).astype(jnp.float...]
    dot_general x1, matrix products: 15.1 us -> 10.6 us  [on_device(): jnp.dot(rows_piece, gate_weights, preferred_element_type=jnp.float32)]
    unnamed x1 -> x3, other arithmetic: 22.6 us -> 22.4 us
  transfers between devices with their start and end apart: 5 -> 19, of which waited for: 5 -> 15; matrix products, arithmetic and copies ran while one was open for 0% -> 3% of each run, Pallas kernels for 0% -> 0%
where the time goes in v1:
time: 377 us; the launch traced here: 375 us
  waiting for transfers between devices  188 us (50%)
  starting transfers between devices  47.1 us (12%)
  matrix products  37.9 us (10%)
  blocking collectives  30.6 us (8%)
  local copies, waits for them, and re-layouts  29.9 us (8%)
  other arithmetic  27.7 us (7%)
  between operations  13.9 us (4%)
    reduce_scatter x1, waiting for transfers between devices, on_device(): lax.psum_scatter(lax.optimization_barrier(partial_value).astype(jnp.float...  79.3 us
    ppermute x8, waiting for transfers between devices, expand_the_edges(): f_now.append(lax.ppermute(f_now[-1], peer_axis, perm=fields))  66.6 us
    ppermute x7, starting transfers between devices, expand_the_edges(): y2.append(lax.ppermute(y2[-1], peer_axis, block_list))  38.9 us
    ppermute x2, waiting for transfers between devices, from_partner(): lax.ppermute(value, axis, [(i, i ^ 1 << stride) for i in range(lax.axis_s...  23.3 us
    unnamed x3, other arithmetic  22.4 us
    unnamed x66, local copies, waits for them, and re-layouts  19.5 us
    psum x1, blocking collectives, on_device(): square_sums = lax.psum(jnp.sum(tokens_f32 * tokens_f32, axis=1), 'expert')  16 us
    all_to_all x1, waiting for transfers between devices, on_device(): lax.all_to_all(chosen, 'expert', split_axis=0, concat_axis=2, tiled=True)[0]  15.8 us
  transfers between devices with their start and end apart: 19, of which 15 were waited for; matrix products, arithmetic and copies ran while one was open for 3% of the time, Pallas kernels for 0%

profile of v1, /device:TPU:0, one launch (start us, length us, event | category | flops | bytes accessed | tf_op | source)
XLA Modules:
  0.0 375.5 jit_solution(10223533661852071113)
XLA Ops:
  8.6 16.0 %psum.7 = f32[256]{0:T(256)S(1)} all-reduce(f32[256]{0:T(256)S(1)} %fusion.14), channel_id=1, replica_groups=mesh['dp'=16,'expert'=8] {'expert'}, use_global_device_ids=true, to_apply=%region_1.2 | all-reduce | flops 256 | bytes 2048 | tf_op jit(solution)/shard_map/psum | solution.py:50
  32.0 15.8 %all-to-all-done = bf16[8,128,512]{2,1,0:T(8,128)(2,1)S(1)} async-done(((bf16[8,128,512]{2,1,0:T(8,128)(2,1)}), bf16[8,128,512]{2,1,0:T(8,128)(2,1)S(1)}, u32[]{:S(2)}, u32[]{:S(2)}) %all-to-all-start) | async-done | bytes 1048608 | tf_op jit(solution)/shard_map/all_to_all | solution.py:60
  51.4 11.6 %collective-permute-done = bf16[64,4096]{1,0:T(8,128)(2,1)S(1)} collective-permute-done((bf16[64,4096]{1,0:T(8,128)(2,1)S(1)}, bf16[64,4096]{1,0:T(8,128)(2,1)S(1)}, u32[]{:S(2)}, u32[]{:S(2)}) %collective-permute-start) | collective-permute-done | bytes 524320 | tf_op jit(solution)/shard_map/ppermute | solution.py:31
  64.7 14.5 %collective-permute-done.1 = bf16[64,4096]{1,0:T(8,128)(2,1)S(1)} collective-permute-done((bf16[64,4096]{1,0:T(8,128)(2,1)S(1)}, bf16[64,4096]{1,0:T(8,128)(2,1)S(1)}, u32[]{:S(2)}, u32[]{:S(2)}) %collective-permute-start.1) | collective-permute-done | bytes 524320 | tf_op jit(solution)/shard_map/ppermute | solution.py:20
  79.3 5.3 %collective-permute-start.9 = (bf16[64,4096]{1,0:T(8,128)(2,1)S(1)}, bf16[64,4096]{1,0:T(8,128)(2,1)S(1)}, u32[]{:S(2)}, u32[]{:S(2)}) collective-permute-start(bf16[64,4096]{1,0:T(8,128)(2,1)S(1)} %add.84), channel_id=1, source_target_pairs={{0,120},{8,0},{16,8},{24,16},{32,24},{40,32},{48,40},{56,48},{64,5... | collective-permute-start | bytes 1572872 | tf_op jit(solution)/shard_map/ppermute | solution.py:22
  84.6 9.8 %collective-permute-done.2 = bf16[64,4096]{1,0:T(8,128)(2,1)S(1)} collective-permute-done((bf16[64,4096]{1,0:T(8,128)(2,1)S(1)}, bf16[64,4096]{1,0:T(8,128)(2,1)S(1)}, u32[]{:S(2)}, u32[]{:S(2)}) %collective-permute-start.2) | collective-permute-done | bytes 524320 | tf_op jit(solution)/shard_map/ppermute | solution.py:20
  94.4 5.3 %collective-permute-start.10 = (bf16[64,4096]{1,0:T(8,128)(2,1)S(1)}, bf16[64,4096]{1,0:T(8,128)(2,1)S(1)}, u32[]{:S(2)}, u32[]{:S(2)}) collective-permute-start(bf16[64,4096]{1,0:T(8,128)(2,1)S(1)} %collective-permute-done.9), channel_id=1, source_target_pairs={{0,120},{8,0},{16,8},{24,16},{32,24},{40,32},{48,40},{56,48},{64,5... | collective-permute-start | bytes 1572872 | tf_op jit(solution)/shard_map/ppermute | solution.py:22
  99.7 8.8 %collective-permute-done.3 = bf16[64,4096]{1,0:T(8,128)(2,1)S(1)} collective-permute-done((bf16[64,4096]{1,0:T(8,128)(2,1)S(1)}, bf16[64,4096]{1,0:T(8,128)(2,1)S(1)}, u32[]{:S(2)}, u32[]{:S(2)}) %collective-permute-start.3) | collective-permute-done | bytes 524320 | tf_op jit(solution)/shard_map/ppermute | solution.py:20
  108.6 5.3 %collective-permute-start.11 = (bf16[64,4096]{1,0:T(8,128)(2,1)S(1)}, bf16[64,4096]{1,0:T(8,128)(2,1)S(1)}, u32[]{:S(2)}, u32[]{:S(2)}) collective-permute-start(bf16[64,4096]{1,0:T(8,128)(2,1)S(1)} %collective-permute-done.10), channel_id=1, source_target_pairs={{0,120},{8,0},{16,8},{24,16},{32,24},{40,32},{48,40},{56,48},{64,5... | collective-permute-start | bytes 1572872 | tf_op jit(solution)/shard_map/ppermute | solution.py:22
  113.9 7.9 %collective-permute-done.4 = bf16[64,4096]{1,0:T(8,128)(2,1)S(1)} collective-permute-done((bf16[64,4096]{1,0:T(8,128)(2,1)S(1)}, bf16[64,4096]{1,0:T(8,128)(2,1)S(1)}, u32[]{:S(2)}, u32[]{:S(2)}) %collective-permute-start.4) | collective-permute-done | bytes 524320 | tf_op jit(solution)/shard_map/ppermute | solution.py:20
  122.7 5.3 %collective-permute-start.12 = (bf16[64,4096]{1,0:T(8,128)(2,1)S(1)}, bf16[64,4096]{1,0:T(8,128)(2,1)S(1)}, u32[]{:S(2)}, u32[]{:S(2)}) collective-permute-start(bf16[64,4096]{1,0:T(8,128)(2,1)S(1)} %collective-permute-done.11), channel_id=1, source_target_pairs={{0,120},{8,0},{16,8},{24,16},{32,24},{40,32},{48,40},{56,48},{64,5... | collective-permute-start | bytes 1572872 | tf_op jit(solution)/shard_map/ppermute | solution.py:22
  128.0 6.3 %collective-permute-done.5 = bf16[64,4096]{1,0:T(8,128)(2,1)S(1)} collective-permute-done((bf16[64,4096]{1,0:T(8,128)(2,1)S(1)}, bf16[64,4096]{1,0:T(8,128)(2,1)S(1)}, u32[]{:S(2)}, u32[]{:S(2)}) %collective-permute-start.5) | collective-permute-done | bytes 524320 | tf_op jit(solution)/shard_map/ppermute | solution.py:20
  135.5 5.8 %collective-permute-start.13 = (bf16[64,4096]{1,0:T(8,128)(2,1)S(1)}, bf16[64,4096]{1,0:T(8,128)(2,1)}, u32[]{:S(2)}, u32[]{:S(2)}) collective-permute-start(bf16[64,4096]{1,0:T(8,128)(2,1)S(1)} %collective-permute-done.12), channel_id=1, source_target_pairs={{0,120},{8,0},{16,8},{24,16},{32,24},{40,32},{48,40},{56,48},{64,5... | collective-permute-start | bytes 1572872 | tf_op jit(solution)/shard_map/ppermute | solution.py:22
  141.3 6.6 %collective-permute-done.6 = bf16[64,4096]{1,0:T(8,128)(2,1)S(1)} collective-permute-done((bf16[64,4096]{1,0:T(8,128)(2,1)S(1)}, bf16[64,4096]{1,0:T(8,128)(2,1)S(1)}, u32[]{:S(2)}, u32[]{:S(2)}) %collective-permute-start.6) | collective-permute-done | bytes 524320 | tf_op jit(solution)/shard_map/ppermute | solution.py:20
  149.1 5.9 %collective-permute-start.14 = (bf16[64,4096]{1,0:T(8,128)(2,1)}, bf16[64,4096]{1,0:T(8,128)(2,1)}, u32[]{:S(2)}, u32[]{:S(2)}) collective-permute-start(bf16[64,4096]{1,0:T(8,128)(2,1)} %collective-permute-done.13), channel_id=1, source_target_pairs={{0,120},{8,0},{16,8},{24,16},{32,24},{40,32},{48,40},{56,48},{64,5... | collective-permute-start | bytes 1572872 | tf_op jit(solution)/shard_map/ppermute | solution.py:22
  155.0 7.4 %collective-permute-done.7 = bf16[64,4096]{1,0:T(8,128)(2,1)} collective-permute-done((bf16[64,4096]{1,0:T(8,128)(2,1)S(1)}, bf16[64,4096]{1,0:T(8,128)(2,1)}, u32[]{:S(2)}, u32[]{:S(2)}) %collective-permute-start.7) | collective-permute-done | bytes 524320 | tf_op jit(solution)/shard_map/ppermute | solution.py:20
  164.2 5.8 %collective-permute-start.15 = (bf16[64,4096]{1,0:T(8,128)(2,1)}, bf16[64,4096]{1,0:T(8,128)(2,1)S(1)}, u32[]{:S(2)}, u32[]{:S(2)}) collective-permute-start(bf16[64,4096]{1,0:T(8,128)(2,1)} %collective-permute-done.14), channel_id=1, source_target_pairs={{0,120},{8,0},{16,8},{24,16},{32,24},{40,32},{48,40},{56,48},{64,5... | collective-permute-start | bytes 1572872 | tf_op jit(solution)/shard_map/ppermute | solution.py:22
  190.4 10.6 %fusion.2 = f32[1024,896]{1,0:T(8,128)} fusion(bf16[2048,4096]{1,0:T(8,128)(2,1)S(1)} %constant_dynamic-update-slice_fusion, s32[]{:T(128)S(6)} %select_n.103, bf16[1,4096,896]{2,1,0:T(8,128)(2,1)S(1)} %bitcast.35), kind=kOutput, calls=%fused_computation.4 | convolution fusion | flops 7516192768 | bytes 19398660 | tf_op jit(solution)/shard_map/dot_general | solution.py:69
  201.0 12.5 %fusion = f32[1024,896]{1,0:T(8,128)} fusion(bf16[2048,4096]{1,0:T(8,128)(2,1)S(1)} %constant_dynamic-update-slice_fusion, s32[]{:T(128)S(6)} %select_n.103, bf16[1,4096,896]{2,1,0:T(8,128)(2,1)} %param.9), kind=kOutput, calls=%fused_computation.2 | convolution fusion | flops 7516192768 | bytes 19398660 | tf_op jit(solution)/shard_map/dot_general | solution.py:70
  213.5 14.3 %convolution_convert_fusion = bf16[1024,4096]{1,0:T(8,128)(2,1)} fusion(bf16[1,896,4096]{2,1,0:T(8,128)(2,1)S(1)} %bitcast.37, f32[1024,896]{1,0:T(8,128)} %fusion, f32[1024,896]{1,0:T(8,128)} %fusion.2), kind=kOutput, calls=%fused_computation.1 | convolution fusion | flops 7525892096 | bytes 23068672 | tf_op jit(solution)/shard_map/dot_general | solution.py:72
  227.9 79.3 %reduce-scatter.2.cloned.1.call-done = bf16[64,4096]{1,0:T(8,128)(2,1)} async-done(((bf16[1024,4096]{1,0:T(8,128)(2,1)}), bf16[64,4096]{1,0:T(8,128)(2,1)}) %reduce-scatter.2.cloned.1.call-update) | async-done | bytes 524304 | tf_op jit(solution)/shard_map/reduce_scatter | solution.py:75
  312.6 22.4 %reduce.10 = bf16[4096,64]{1,0:T(8,128)(2,1)S(1)} reduce(bf16[4096,1,64]{2,1,0:T(2,128)(2,1)S(1)} %bitcast.27, bf16[]{:T(256)} %broadcast.171), dimensions={1}, to_apply=%bitcast.23.reduce_sub_computation | reduce | bytes 1048578
  335.7 14.7 %all_to_all.27 = bf16[8,2,16384]{2,1,0:T(2,128)(2,1)S(1)} all-to-all(bf16[8,2,16384]{2,1,0:T(2,128)(2,1)S(1)} %reshape.126), channel_id=1, replica_groups=mesh['dp'=16,'expert'=8] {'expert'}, dimensions={0} | all-to-all | bytes 1048576 | tf_op jit(solution)/shard_map/all_to_all | solution.py:81
  355.7 11.7 %collective-permute-done.16 = bf16[64,8,512]{2,1,0:T(8,128)(2,1)S(1)} collective-permute-done((bf16[64,8,512]{2,1,0:T(8,128)(2,1)S(1)}, bf16[64,8,512]{2,1,0:T(8,128)(2,1)S(1)}, u32[]{:S(2)}, u32[]{:S(2)}) %collective-permute-start.16) | collective-permute-done | bytes 524320 | tf_op jit(solution)/shard_map/ppermute | solution.py:31
  (109 shorter events, 52.3 us)
Async XLA Ops:
  6.5 349.0 %copy-start = (f32[8,8]{1,0:T(8,128)S(1)}, f32[8,8]{1,0:T(8,128)}, u32[]{:S(2)}) copy-start(f32[8,8]{1,0:T(8,128)} %param.13) | copy-start | bytes 772
  28.4 19.4 %all-to-all-start = ((bf16[8,128,512]{2,1,0:T(8,128)(2,1)}), bf16[8,128,512]{2,1,0:T(8,128)(2,1)S(1)}, u32[]{:S(2)}, u32[]{:S(2)}) async-start(bf16[8,128,512]{2,1,0:T(8,128)(2,1)} %select_select_fusion), calls=%async_computation | async-start | bytes 2097152 | tf_op jit(solution)/shard_map/all_to_all | solution.py:60
  31.9 275.3 %reduce-scatter.2.cloned.1.call-start = ((), (), s32[]{:S(2)}) async-start(), calls=%async_computation.3 | async-start | bytes 8912896 | tf_op jit(solution)/shard_map/reduce_scatter | solution.py:75
  49.5 13.5 %collective-permute-start = (bf16[64,4096]{1,0:T(8,128)(2,1)S(1)}, bf16[64,4096]{1,0:T(8,128)(2,1)S(1)}, u32[]{:S(2)}, u32[]{:S(2)}) collective-permute-start(bf16[64,4096]{1,0:T(8,128)(2,1)S(1)} %copy.91), channel_id=1, source_target_pairs={{0,8},{8,0},{16,24},{24,16},{32,40},{40,32},{48,56},{56,48},{64,72... | collective-permute-start | bytes 1572872 | tf_op jit(solution)/shard_map/ppermute | solution.py:31
  63.2 16.1 %collective-permute-start.1 = (bf16[64,4096]{1,0:T(8,128)(2,1)S(1)}, bf16[64,4096]{1,0:T(8,128)(2,1)S(1)}, u32[]{:S(2)}, u32[]{:S(2)}) collective-permute-start(bf16[64,4096]{1,0:T(8,128)(2,1)S(1)} %add.84), channel_id=1, source_target_pairs={{0,8},{8,16},{16,24},{24,32},{32,40},{40,48},{48,56},{56,64},{64,7... | collective-permute-start | bytes 1572872 | tf_op jit(solution)/shard_map/ppermute | solution.py:20
  79.3 15.1 %collective-permute-start.2 = (bf16[64,4096]{1,0:T(8,128)(2,1)S(1)}, bf16[64,4096]{1,0:T(8,128)(2,1)S(1)}, u32[]{:S(2)}, u32[]{:S(2)}) collective-permute-start(bf16[64,4096]{1,0:T(8,128)(2,1)S(1)} %collective-permute-done.1), channel_id=1, source_target_pairs={{0,8},{8,16},{16,24},{24,32},{32,40},{40,48},{48,56},{56,64},{64,7... | collective-permute-start | bytes 1572872 | tf_op jit(solution)/shard_map/ppermute | solution.py:20
  79.3 15.1 %collective-permute-start.9 = (bf16[64,4096]{1,0:T(8,128)(2,1)S(1)}, bf16[64,4096]{1,0:T(8,128)(2,1)S(1)}, u32[]{:S(2)}, u32[]{:S(2)}) collective-permute-start(bf16[64,4096]{1,0:T(8,128)(2,1)S(1)} %add.84), channel_id=1, source_target_pairs={{0,120},{8,0},{16,8},{24,16},{32,24},{40,32},{48,40},{56,48},{64,5... | collective-permute-start | bytes 1572872 | tf_op jit(solution)/shard_map/ppermute | solution.py:22
  94.4 14.2 %collective-permute-start.3 = (bf16[64,4096]{1,0:T(8,128)(2,1)S(1)}, bf16[64,4096]{1,0:T(8,128)(2,1)S(1)}, u32[]{:S(2)}, u32[]{:S(2)}) collective-permute-start(bf16[64,4096]{1,0:T(8,128)(2,1)S(1)} %collective-permute-done.2), channel_id=1, source_target_pairs={{0,8},{8,16},{16,24},{24,32},{32,40},{40,48},{48,56},{56,64},{64,7... | collective-permute-start | bytes 1572872 | tf_op jit(solution)/shard_map/ppermute | solution.py:20
  94.4 14.2 %collective-permute-start.10 = (bf16[64,4096]{1,0:T(8,128)(2,1)S(1)}, bf16[64,4096]{1,0:T(8,128)(2,1)S(1)}, u32[]{:S(2)}, u32[]{:S(2)}) collective-permute-start(bf16[64,4096]{1,0:T(8,128)(2,1)S(1)} %collective-permute-done.9), channel_id=1, source_target_pairs={{0,120},{8,0},{16,8},{24,16},{32,24},{40,32},{48,40},{56,48},{64,5... | collective-permute-start | bytes 1572872 | tf_op jit(solution)/shard_map/ppermute | solution.py:22
  108.6 13.3 %collective-permute-start.4 = (bf16[64,4096]{1,0:T(8,128)(2,1)S(1)}, bf16[64,4096]{1,0:T(8,128)(2,1)S(1)}, u32[]{:S(2)}, u32[]{:S(2)}) collective-permute-start(bf16[64,4096]{1,0:T(8,128)(2,1)S(1)} %collective-permute-done.3), channel_id=1, source_target_pairs={{0,8},{8,16},{16,24},{24,32},{32,40},{40,48},{48,56},{56,64},{64,7... | collective-permute-start | bytes 1572872 | tf_op jit(solution)/shard_map/ppermute | solution.py:20
  108.6 13.3 %collective-permute-start.11 = (bf16[64,4096]{1,0:T(8,128)(2,1)S(1)}, bf16[64,4096]{1,0:T(8,128)(2,1)S(1)}, u32[]{:S(2)}, u32[]{:S(2)}) collective-permute-start(bf16[64,4096]{1,0:T(8,128)(2,1)S(1)} %collective-permute-done.10), channel_id=1, source_target_pairs={{0,120},{8,0},{16,8},{24,16},{32,24},{40,32},{48,40},{56,48},{64,5... | collective-permute-start | bytes 1572872 | tf_op jit(solution)/shard_map/ppermute | solution.py:22
  121.8 27.3 %copy-start.5 = (bf16[64,4096]{1,0:T(8,128)(2,1)}, bf16[64,4096]{1,0:T(8,128)(2,1)S(1)}, u32[]{:S(2)}) copy-start(bf16[64,4096]{1,0:T(8,128)(2,1)S(1)} %collective-permute-done.4) | copy-start | bytes 1572868
  121.8 12.5 %collective-permute-start.5 = (bf16[64,4096]{1,0:T(8,128)(2,1)S(1)}, bf16[64,4096]{1,0:T(8,128)(2,1)S(1)}, u32[]{:S(2)}, u32[]{:S(2)}) collective-permute-start(bf16[64,4096]{1,0:T(8,128)(2,1)S(1)} %collective-permute-done.4), channel_id=1, source_target_pairs={{0,8},{8,16},{16,24},{24,32},{32,40},{40,48},{48,56},{56,64},{64,7... | collective-permute-start | bytes 1572872 | tf_op jit(solution)/shard_map/ppermute | solution.py:20
  122.7 12.0 %collective-permute-start.12 = (bf16[64,4096]{1,0:T(8,128)(2,1)S(1)}, bf16[64,4096]{1,0:T(8,128)(2,1)S(1)}, u32[]{:S(2)}, u32[]{:S(2)}) collective-permute-start(bf16[64,4096]{1,0:T(8,128)(2,1)S(1)} %collective-permute-done.11), channel_id=1, source_target_pairs={{0,120},{8,0},{16,8},{24,16},{32,24},{40,32},{48,40},{56,48},{64,5... | collective-permute-start | bytes 1572872 | tf_op jit(solution)/shard_map/ppermute | solution.py:22
  134.3 13.6 %collective-permute-start.6 = (bf16[64,4096]{1,0:T(8,128)(2,1)S(1)}, bf16[64,4096]{1,0:T(8,128)(2,1)S(1)}, u32[]{:S(2)}, u32[]{:S(2)}) collective-permute-start(bf16[64,4096]{1,0:T(8,128)(2,1)S(1)} %collective-permute-done.5), channel_id=1, source_target_pairs={{0,8},{8,16},{16,24},{24,32},{32,40},{40,48},{48,56},{56,64},{64,7... | collective-permute-start | bytes 1572872 | tf_op jit(solution)/shard_map/ppermute | solution.py:20
  135.5 13.6 %collective-permute-start.13 = (bf16[64,4096]{1,0:T(8,128)(2,1)S(1)}, bf16[64,4096]{1,0:T(8,128)(2,1)}, u32[]{:S(2)}, u32[]{:S(2)}) collective-permute-start(bf16[64,4096]{1,0:T(8,128)(2,1)S(1)} %collective-permute-done.12), channel_id=1, source_target_pairs={{0,120},{8,0},{16,8},{24,16},{32,24},{40,32},{48,40},{56,48},{64,5... | collective-permute-start | bytes 1572872 | tf_op jit(solution)/shard_map/ppermute | solution.py:22
  147.9 14.4 %collective-permute-start.7 = (bf16[64,4096]{1,0:T(8,128)(2,1)S(1)}, bf16[64,4096]{1,0:T(8,128)(2,1)}, u32[]{:S(2)}, u32[]{:S(2)}) collective-permute-start(bf16[64,4096]{1,0:T(8,128)(2,1)S(1)} %collective-permute-done.6), channel_id=1, source_target_pairs={{0,8},{8,16},{16,24},{24,32},{32,40},{40,48},{48,56},{56,64},{64,7... | collective-permute-start | bytes 1572872 | tf_op jit(solution)/shard_map/ppermute | solution.py:20
  149.1 15.1 %collective-permute-start.14 = (bf16[64,4096]{1,0:T(8,128)(2,1)}, bf16[64,4096]{1,0:T(8,128)(2,1)}, u32[]{:S(2)}, u32[]{:S(2)}) collective-permute-start(bf16[64,4096]{1,0:T(8,128)(2,1)} %collective-permute-done.13), channel_id=1, source_target_pairs={{0,120},{8,0},{16,8},{24,16},{32,24},{40,32},{48,40},{56,48},{64,5... | collective-permute-start | bytes 1572872 | tf_op jit(solution)/shard_map/ppermute | solution.py:22
  162.4 12.8 %collective-permute-start.8 = (bf16[64,4096]{1,0:T(8,128)(2,1)}, bf16[64,4096]{1,0:T(8,128)(2,1)}, u32[]{:S(2)}, u32[]{:S(2)}) collective-permute-start(bf16[64,4096]{1,0:T(8,128)(2,1)} %collective-permute-done.7), channel_id=1, source_target_pairs={{0,8},{8,16},{16,24},{24,32},{32,40},{40,48},{48,56},{56,64},{64,7... | collective-permute-start | bytes 1572872 | tf_op jit(solution)/shard_map/ppermute | solution.py:20
  162.4 25.6 %copy-start.2 = (bf16[64,4096]{1,0:T(8,128)(2,1)S(1)}, bf16[64,4096]{1,0:T(8,128)(2,1)}, u32[]{:S(2)}) copy-start(bf16[64,4096]{1,0:T(8,128)(2,1)} %copy-done.1) | copy-start | bytes 1572868
  162.4 25.6 %copy-start.4 = (bf16[64,4096]{1,0:T(8,128)(2,1)S(1)}, bf16[64,4096]{1,0:T(8,128)(2,1)}, u32[]{:S(2)}) copy-start(bf16[64,4096]{1,0:T(8,128)(2,1)} %copy-done.3) | copy-start | bytes 1572868
  162.4 27.9 %slice-start = ((s8[7340032]{0:T(1024)(128)(4,1)}), s8[4194304]{0:T(1024)(128)(4,1)S(1)}, s32[]{:S(2)}) async-start(s8[7340032]{0:T(1024)(128)(4,1)} %bitcast.34), calls=%async_computation.4 | async-start | bytes 8388608
  164.2 21.0 %collective-permute-start.15 = (bf16[64,4096]{1,0:T(8,128)(2,1)}, bf16[64,4096]{1,0:T(8,128)(2,1)S(1)}, u32[]{:S(2)}, u32[]{:S(2)}) collective-permute-start(bf16[64,4096]{1,0:T(8,128)(2,1)} %collective-permute-done.14), channel_id=1, source_target_pairs={{0,120},{8,0},{16,8},{24,16},{32,24},{40,32},{48,40},{56,48},{64,5... | collective-permute-start | bytes 1572872 | tf_op jit(solution)/shard_map/ppermute | solution.py:22
  354.1 13.4 %collective-permute-start.16 = (bf16[64,8,512]{2,1,0:T(8,128)(2,1)S(1)}, bf16[64,8,512]{2,1,0:T(8,128)(2,1)S(1)}, u32[]{:S(2)}, u32[]{:S(2)}) collective-permute-start(bf16[64,8,512]{2,1,0:T(8,128)(2,1)S(1)} %bitcast.32), channel_id=1, source_target_pairs={{0,8},{8,0},{16,24},{24,16},{32,40},{40,32},{48,56},{56,48},{64,72... | collective-permute-start | bytes 1572872 | tf_op jit(solution)/shard_map/ppermute | solution.py:31
  (10 other events, 153.3 us)
Sparse Core Ops, SparseCore 0:
  228.0 79.1 reduce-scatter.1
